TPU v7x, 32 devices: a whole 2x2x4 slice. The times are simulated.
32 devices in a mesh: row: 8 (over z, x), col: 4 (over y, core).
Axes of the slice: x: 2, y: 2, z: 4, core: 2. Of those that a mesh axis runs over, the one named last changes fastest.
Arguments:
- innovations: float32 [64, 16384], P(None, ('row', 'col')), may hold values from -300 to 300
- obs_factors: float32 [64, 16384], P(None, ('row', 'col')), may hold values from -6 to 6
- component: int32 [16384], P(('row', 'col')), may hold values 0 or 1
- obs_error: float32 [16384], P(('row', 'col')), may hold values from 0.5 to 2
- coupling: float32 [2, 2], replicated, may hold values from 0.5 to 2
- tile_slots: int32 [8, 4, 8, 3], P('row', 'col'), may hold values from 0 to 7, as said below
Outputs:
- increment: float32 [64, 16384], P(None, ('row', 'col'))
- residual: float32 [64, 16384], P(None, ('row', 'col'))
Inputs may be any that keep to these rules, and one draw needn't show every extreme that they name: `tile_slots`: each device's slots name distinct (local block row, local block column) pairs; on some device all 8 slots are live; the live flag is 0 or 1; local block rows are below 4 and local block columns below 8.
All inputs are finite; a program needn't handle non-finite values. No bound on the sum of `component` on one device may be relied on, other than what follows from the above.
Results may differ from a plain program's by a relative error of at most 0.0003.
Values sent between devices are 32-bit elements; how exact they have to be, the bound alone decides.
A program may use at most 64 MiB of HBM per device.

v0:
```python
import jax
import jax.numpy as jnp
from jax import lax
from jax.sharding import PartitionSpec as P

TILE = 512
ITERS = 3
length_sq = 12.0


def tile_matrix(left_factors, right_factors, left_labels, right_labels, coupling):
    left_norms = jnp.sum(left_factors * left_factors, axis=0)
    right_norms = jnp.sum(right_factors * right_factors, axis=0)
    products = lax.dot_general(
        left_factors,
        right_factors,
        (((0,), (0,)), ((), ())),
        precision=lax.Precision.HIGHEST,
        preferred_element_type=jnp.float32,
    )
    pair_coupling = (1.0 - left_labels)[:, None] * (
        (1.0 - right_labels)[None, :] * coupling[0, 0] + right_labels[None, :] * coupling[0, 1]
    ) + left_labels[:, None] * (
        (1.0 - right_labels)[None, :] * coupling[1, 0] + right_labels[None, :] * coupling[1, 1]
    )
    return pair_coupling * jnp.exp(
        -(left_norms[:, None] + right_norms[None, :] - 2.0 * products) / length_sq
    )


def take_segment(array, block):
    start = block * TILE
    return lax.dynamic_slice_in_dim(array, start, TILE, array.ndim - 1)


def add_segment(vector, block, values):
    start = block * TILE
    last_axis = vector.ndim - 1
    before = lax.dynamic_slice_in_dim(vector, start, TILE, last_axis)
    return lax.dynamic_update_slice_in_dim(vector, before + values, start, last_axis)


def squares(residual):
    return lax.psum(jnp.sum(residual * residual, axis=1), ("row", "col"))


def shards(innovations, obs_factors, component, obs_error, coupling, tile_slots):
    labels_float = component.astype(jnp.float32)
    row_factors, row_labels = (
        lax.all_gather(obs_factors, "col", axis=1, tiled=True),
        lax.all_gather(labels_float, "col", axis=0, tiled=True),
    )
    column_factors, column_labels = (
        lax.all_gather(obs_factors, "row", axis=1, tiled=True),
        lax.all_gather(labels_float, "row", axis=0, tiled=True),
    )
    slots = tile_slots[0, 0]
    count = slots.shape[0]
    flags = slots[:, 2].astype(jnp.float32)
    rhs_count = innovations.shape[0]

    def make_tile(number):
        row_block = slots[number, 0]
        column_block = slots[number, 1]
        block_matrix = tile_matrix(
            take_segment(row_factors, row_block),
            take_segment(column_factors, column_block),
            take_segment(row_labels, row_block),
            take_segment(column_labels, column_block),
            coupling,
        )
        return block_matrix * flags[number]

    def visit(totals, work):
        result = work(totals)
        return result

    stored = jnp.zeros((count, TILE, TILE), jnp.float32)

    def weigh(number, carry):

        def work(carry):
            row_totals, column_totals, stored = carry
            block_matrix = make_tile(number)
            row_totals = add_segment(row_totals, slots[number, 0], jnp.sum(block_matrix, axis=1))
            column_totals = add_segment(
                column_totals, slots[number, 1], jnp.sum(block_matrix, axis=0)
            )
            stored = lax.dynamic_update_index_in_dim(stored, block_matrix, number, 0)
            return (row_totals, column_totals, stored)

        return visit(carry, work)

    start_carry = (
        jnp.zeros((row_factors.shape[1],), jnp.float32),
        jnp.zeros((column_factors.shape[1],), jnp.float32),
        stored,
    )
    row_totals, column_totals, stored = lax.fori_loop(0, count, weigh, start_carry)
    diagonal = (
        obs_error
        + lax.psum_scatter(row_totals, "col", scatter_dimension=0, tiled=True)
        + lax.psum_scatter(column_totals, "row", scatter_dimension=0, tiled=True)
    )

    def fetch(number):
        block_matrix = lax.dynamic_index_in_dim(stored, number, 0, keepdims=False)
        return block_matrix

    increment = jnp.zeros_like(innovations)
    residual = innovations
    direction = innovations
    norm_now = squares(residual)
    for repeat in range(ITERS):
        column_values = lax.all_gather(direction, "row", axis=1, tiled=True)
        row_values = lax.all_gather(direction, "col", axis=1, tiled=True)

        def sweep(number, carry):

            def work(carry):
                row_image, column_image = carry
                block_matrix = fetch(number)
                row_block = slots[number, 0]
                column_block = slots[number, 1]
                right_part = lax.dot_general(
                    take_segment(column_values, column_block),
                    block_matrix,
                    (((1,), (1,)), ((), ())),
                    precision=lax.Precision.HIGHEST,
                    preferred_element_type=jnp.float32,
                )
                left_part = jnp.dot(
                    take_segment(row_values, row_block),
                    block_matrix,
                    precision=lax.Precision.HIGHEST,
                    preferred_element_type=jnp.float32,
                )
                return (
                    add_segment(row_image, row_block, right_part),
                    add_segment(column_image, column_block, left_part),
                )

            return visit(carry, work)

        start_image = (
            jnp.zeros((rhs_count, row_values.shape[1]), jnp.float32),
            jnp.zeros((rhs_count, column_values.shape[1]), jnp.float32),
        )
        row_image, column_image = lax.fori_loop(0, count, sweep, start_image)
        image = (
            diagonal[None, :] * direction
            + lax.psum_scatter(row_image, "col", scatter_dimension=1, tiled=True)
            + lax.psum_scatter(column_image, "row", scatter_dimension=1, tiled=True)
        )
        alpha = norm_now / lax.psum(jnp.sum(direction * image, axis=1), ("row", "col"))
        increment = increment + alpha[:, None] * direction
        residual = residual - alpha[:, None] * image
        norm_next = squares(residual)
        direction = residual + (norm_next / norm_now)[:, None] * direction
        norm_now = norm_next
    return (increment, residual)


def solution(mesh):
    return jax.shard_map(
        shards,
        mesh=mesh,
        in_specs=(
            P(None, ("row", "col")),
            P(None, ("row", "col")),
            P(("row", "col")),
            P(("row", "col")),
            P(),
            P("row", "col", None, None),
        ),
        out_specs=(P(None, ("row", "col")), P(None, ("row", "col"))),
        check_vma=False,
    )
```

profile of v0, /device:TPU:0, one launch (start us, length us, event | category | flops | bytes accessed | tf_op | source)
XLA Modules:
  0.0 869.6 jit_solution(11168833523570514415)
XLA Ops:
  9.4 28.0 %all-gather.1 = f32[8,1,512]{2,1,0:T(1,128)S(1)} all-gather(f32[1,1,512]{2,1,0:T(1,128)S(1)} %bitcast.84), channel_id=1, replica_groups=mesh['row'=8,'col'=4] {'row'}, dimensions={0}, use_global_device_ids=true | all-gather | bytes 18432 | tf_op jit(solution)/shard_map/all_gather | solution.py:55
  37.4 5.2 all-gather
  42.6 7.5 all_gather.32
  50.0 7.5 all_gather.35
  58.2 95.6 %while.62 = (s32[]{:T(128)}, f32[2048]{0:T(1024)S(1)}, f32[4096]{0:T(1024)S(1)}, f32[8,512,512]{2,1,0:T(8,128)}, s32[8,3]{0,1:T(4,128)S(1)}, /*index=5*/f32[2048...) while((s32[]{:T(128)}, f32[2048]{0:T(1024)S(1)}, ...), condition=%wide.region_7.8_spmd, body=%wide.region_2.7_spmd.sunk | while | flops 204606480 | bytes 3716449 | solution.py:99
  61.6 2.6 multiply_add_fusion.6
  65.8 3.0 fusion.62
  73.5 2.6 multiply_add_fusion.6
  77.7 3.1 fusion.62
  85.6 2.6 multiply_add_fusion.6
  89.7 3.0 fusion.62
  97.5 2.6 multiply_add_fusion.6
  101.7 3.0 fusion.62
  109.4 2.6 multiply_add_fusion.6
  113.6 3.0 fusion.62
  121.4 2.6 multiply_add_fusion.6
  125.5 3.0 fusion.62
  133.3 2.6 multiply_add_fusion.6
  137.5 3.0 fusion.62
  145.3 2.6 multiply_add_fusion.6
  149.5 3.0 fusion.62
  154.0 50.7 %while.63 = (s32[]{:T(128)}, f32[64,2048]{1,0:T(8,128)S(1)}, f32[64,4096]{1,0:T(8,128)S(1)}, s32[8,3]{0,1:T(4,128)S(1)}, f32[64,4096]{1,0:T(8,128)}, /*index=5*/...) while((s32[]{:T(128)}, f32[64,2048]{1,0:T(8,128)S(1)}, ...), condition=%wide.region_11.12_spmd, body=%wide.region_10.11_spmd.sunk | while | flops 402718720 | bytes 2884853 | solution.py:149
  170.6 2.4 fusion.67
  202.3 2.4 fusion.67
  208.7 35.7 %all-reduce.1 = f32[4096]{0:T(1024)S(1)} all-reduce(f32[4096]{0:T(1024)S(1)} %get-tuple-element.564), channel_id=3, replica_groups=mesh['row'=8,'col'=4] {'row'}, use_global_device_ids=true, to_apply=%region_9.10.clone | all-reduce | flops 4096 | bytes 32768
  244.3 6.1 all-reduce
  250.6 44.0 %reduce-scatter.9.cloned.1.call-done = f32[64,512]{1,0:T(8,128)} async-done(((f32[64,4096]{1,0:T(8,128)}), f32[64,512]{1,0:T(8,128)}) %reduce-scatter.9.cloned.1.call-update) | async-done | bytes 131088 | tf_op jit(solution)/shard_map/reduce_scatter | solution.py:153
  295.7 39.8 %all-reduce.2 = (f32[64]{0:T(128)S(1)}, f32[64]{0:T(128)S(1)}) all-reduce(f32[64]{0:T(128)S(1)} %get-tuple-element.575, f32[64]{0:T(128)S(1)} %get-tuple-element.574), channel_id=1, replica_groups=mesh['row'=8,'col'=4] {'row','col'}, use_global_device_ids=true, to_apply=%region_1.2 | all-reduce | flops 128 | bytes 1024 | tf_op jit(solution)/shard_map/psum | solution.py:44
  336.7 39.3 %psum.44 = f32[64]{0:T(128)S(1)} all-reduce(f32[64]{0:T(128)S(1)} %get-tuple-element.646), channel_id=1, replica_groups=mesh['row'=8,'col'=4] {'row','col'}, use_global_device_ids=true, to_apply=%region_17.18 | all-reduce | flops 64 | bytes 512 | tf_op jit(solution)/shard_map/psum | solution.py:44
  376.8 8.2 all_gather.37
  384.9 32.0 %all-gather.11.cloned.1.call-done = f32[64,4096]{1,0:T(8,128)} async-done(((f32[64,512]{1,0:T(8,128)}), f32[64,4096]{1,0:T(8,128)}) %all-gather.11.cloned.1.call-update) | async-done | bytes 1048592 | tf_op jit(solution)/shard_map/all_gather | solution.py:115
  417.1 51.1 %while.64 = (s32[]{:T(128)}, f32[64,2048]{1,0:T(8,128)S(1)}, f32[64,4096]{1,0:T(8,128)S(1)}, s32[8,3]{0,1:T(4,128)S(1)}, f32[64,4096]{1,0:T(8,128)}, /*index=5*/...) while((s32[]{:T(128)}, f32[64,2048]{1,0:T(8,128)S(1)}, ...), condition=%wide.region_19.20_spmd, body=%wide.region_18.19_spmd.sunk | while | flops 402718720 | bytes 2884853 | solution.py:149
  433.8 2.4 fusion.73
  453.0 2.4 fusion.73
  465.8 2.4 fusion.73
  469.8 19.7 %reduce-scatter.11.cloned.1.call-done = f32[64,512]{1,0:T(8,128)} async-done(((f32[64,2048]{1,0:T(8,128)}), f32[64,512]{1,0:T(8,128)}) %reduce-scatter.11.cloned.1.call-update) | async-done | bytes 131088 | tf_op jit(solution)/shard_map/reduce_scatter | solution.py:152
  489.5 68.0 %reduce-scatter.13.cloned.1.call-done = f32[64,512]{1,0:T(8,128)} async-done(((f32[64,4096]{1,0:T(8,128)}), f32[64,512]{1,0:T(8,128)}) %reduce-scatter.13.cloned.1.call-update) | async-done | bytes 131088 | tf_op jit(solution)/shard_map/reduce_scatter | solution.py:153
  558.6 39.9 %psum.45 = f32[64]{0:T(128)S(1)} all-reduce(f32[64]{0:T(128)S(1)} %multiply_reduce_fusion.4), channel_id=1, replica_groups=mesh['row'=8,'col'=4] {'row','col'}, use_global_device_ids=true, to_apply=%region_23.24 | all-reduce | flops 64 | bytes 512 | tf_op jit(solution)/shard_map/psum | solution.py:155
  599.7 39.3 %psum.46 = f32[64]{0:T(128)S(1)} all-reduce(f32[64]{0:T(128)S(1)} %get-tuple-element.644), channel_id=1, replica_groups=mesh['row'=8,'col'=4] {'row','col'}, use_global_device_ids=true, to_apply=%region_25.26 | all-reduce | flops 64 | bytes 512 | tf_op jit(solution)/shard_map/psum | solution.py:44
  639.7 8.3 all_gather.39
  648.1 31.8 %all-gather.13.cloned.1.call-done = f32[64,4096]{1,0:T(8,128)} async-done(((f32[64,512]{1,0:T(8,128)}), f32[64,4096]{1,0:T(8,128)}) %all-gather.13.cloned.1.call-update) | async-done | bytes 1048592 | tf_op jit(solution)/shard_map/all_gather | solution.py:115
  680.0 51.1 %while.65 = (s32[]{:T(128)}, f32[64,2048]{1,0:T(8,128)S(1)}, f32[64,4096]{1,0:T(8,128)S(1)}, s32[8,3]{0,1:T(4,128)S(1)}, f32[64,4096]{1,0:T(8,128)}, /*index=5*/...) while((s32[]{:T(128)}, f32[64,2048]{1,0:T(8,128)S(1)}, ...), condition=%wide.region_27.28_spmd, body=%wide.region_26.27_spmd.sunk | while | flops 402718720 | bytes 2884853 | solution.py:149
  684.0 2.4 fusion.79
  703.1 2.4 fusion.79
  722.3 2.4 fusion.79
  732.5 19.9 %reduce-scatter.15.cloned.1.call-done = f32[64,512]{1,0:T(8,128)} async-done(((f32[64,2048]{1,0:T(8,128)}), f32[64,512]{1,0:T(8,128)}) %reduce-scatter.15.cloned.1.call-update) | async-done | bytes 131088 | tf_op jit(solution)/shard_map/reduce_scatter | solution.py:152
  752.4 67.6 %reduce-scatter.17.cloned.1.call-done = f32[64,512]{1,0:T(8,128)} async-done(((f32[64,4096]{1,0:T(8,128)}), f32[64,512]{1,0:T(8,128)}) %reduce-scatter.17.cloned.1.call-update) | async-done | bytes 131088 | tf_op jit(solution)/shard_map/reduce_scatter | solution.py:153
  821.1 39.9 %psum.47 = f32[64]{0:T(128)S(1)} all-reduce(f32[64]{0:T(128)S(1)} %multiply_reduce_fusion.2), channel_id=1, replica_groups=mesh['row'=8,'col'=4] {'row','col'}, use_global_device_ids=true, to_apply=%region_31.32 | all-reduce | flops 64 | bytes 512 | tf_op jit(solution)/shard_map/psum | solution.py:155
  (195 shorter events, 160.5 us)
Async XLA Ops:
  7.2 51.0 %all-gather.7.cloned.1.call-start = ((), (), s32[]{:S(2)}) async-start(), calls=%async_computation.6 | async-start | bytes 1179648 | tf_op jit(solution)/shard_map/all_gather | solution.py:54
  7.9 146.0 %all-gather.9.cloned.1.call-start = ((), (), s32[]{:S(2)}) async-start(), calls=%async_computation.7 | async-start | bytes 1179648 | tf_op jit(solution)/shard_map/all_gather | solution.py:115
  8.6 241.9 %reduce-scatter.7.cloned.1.call-start = ((), (), s32[]{:S(2)}) async-start(), calls=%async_computation.8 | async-start | bytes 655360 | tf_op jit(solution)/shard_map/reduce_scatter | solution.py:152
  153.9 52.3 %copy-start.11 = (u32[32]{0:T(128)S(1)}, u32[32]{0:T(128)}, u32[]{:S(2)}) copy-start(u32[32]{0:T(128)} %constant.217) | copy-start | bytes 388
  154.0 52.8 %copy-start.10 = (u32[32]{0:T(128)S(1)}, u32[32]{0:T(128)}, u32[]{:S(2)}) copy-start(u32[32]{0:T(128)} %constant.221) | copy-start | bytes 388
  154.0 96.5 %copy-start.9 = (f32[512]{0:T(512)S(1)}, f32[512]{0:T(512)}, u32[]{:S(2)}) copy-start(f32[512]{0:T(512)} %param.17) | copy-start | bytes 6148
  154.0 140.6 %copy-start.7 = (f32[64,512]{1,0:T(8,128)S(1)}, f32[64,512]{1,0:T(8,128)}, u32[]{:S(2)}) copy-start(f32[64,512]{1,0:T(8,128)} %param.14) | copy-start | bytes 393220
  204.7 0.8 copy-start.5
  204.8 1.2 copy-start.1
  205.6 89.0 %reduce-scatter.9.cloned.1.call-start = ((), (), s32[]{:S(2)}) async-start(), calls=%async_computation.9 | async-start | bytes 1179648 | tf_op jit(solution)/shard_map/reduce_scatter | solution.py:153
  206.1 210.8 %all-gather.11.cloned.1.call-start = ((), (), s32[]{:S(2)}) async-start(), calls=%async_computation.10 | async-start | bytes 1179648 | tf_op jit(solution)/shard_map/all_gather | solution.py:115
  376.7 112.8 %reduce-scatter.11.cloned.1.call-start = ((), (), s32[]{:S(2)}) async-start(), calls=%async_computation.11 | async-start | bytes 655360 | tf_op jit(solution)/shard_map/reduce_scatter | solution.py:152
  417.0 140.5 %copy-start.3 = (f32[64,512]{1,0:T(8,128)S(1)}, f32[64,512]{1,0:T(8,128)}, u32[]{:S(2)}) copy-start(f32[64,512]{1,0:T(8,128)} %multiply_add_fusion.4) | copy-start | bytes 393220
  468.2 0.8 copy-start.6
  468.2 1.2 copy-start.2
  469.0 88.5 %reduce-scatter.13.cloned.1.call-start = ((), (), s32[]{:S(2)}) async-start(), calls=%async_computation.12 | async-start | bytes 1179648 | tf_op jit(solution)/shard_map/reduce_scatter | solution.py:153
  469.8 210.1 %all-gather.13.cloned.1.call-start = ((), (), s32[]{:S(2)}) async-start(), calls=%async_computation.13 | async-start | bytes 1179648 | tf_op jit(solution)/shard_map/all_gather | solution.py:115
  639.7 112.7 %reduce-scatter.15.cloned.1.call-start = ((), (), s32[]{:S(2)}) async-start(), calls=%async_computation.14 | async-start | bytes 655360 | tf_op jit(solution)/shard_map/reduce_scatter | solution.py:152
  679.9 140.1 %copy-start.8 = (f32[64,512]{1,0:T(8,128)S(1)}, f32[64,512]{1,0:T(8,128)}, u32[]{:S(2)}) copy-start(f32[64,512]{1,0:T(8,128)} %multiply_add_fusion.3) | copy-start | bytes 393220
  731.1 0.8 copy-start.4
  731.1 1.2 copy-start
  731.9 88.1 %reduce-scatter.17.cloned.1.call-start = ((), (), s32[]{:S(2)}) async-start(), calls=%async_computation.15 | async-start | bytes 1179648 | tf_op jit(solution)/shard_map/reduce_scatter | solution.py:153
Sparse Core Ops, SparseCore 0:
  10.2 42.9 all-gather.6
  55.3 38.9 all-gather.8
  205.7 20.9 reduce-scatter.6
  230.0 64.5 reduce-scatter.8
  376.9 40.0 all-gather.10
  469.1 20.3 reduce-scatter.10
  492.9 64.5 reduce-scatter.12
  639.8 40.0 all-gather.12
  732.1 20.3 reduce-scatter.14
  755.7 64.2 reduce-scatter.16
where the time goes:
time: 873 us; the launch traced here: 870 us
  blocking collectives  305 us (35%)
  waiting for transfers between devices  285 us (33%)
  matrix products  130 us (15%)
  local copies, waits for them, and re-layouts  52 us (6%)
  loops' own time  41.6 us (5%)
  other arithmetic  40.3 us (5%)
  between operations  15.7 us (2%)
    reduce_scatter x3, waiting for transfers between devices, shards(): lax.psum_scatter(column_image, 'row', scatter_dimension=1, tiled=True)  180 us
    psum x3, blocking collectives, squares(): return lax.psum(jnp.sum(residual * residual, axis=1), ('row', 'col'))  118 us
    psum x2, blocking collectives, shards(): lax.psum(jnp.sum(direction * image, axis=1), ('row', 'col'))  79.7 us
    all_gather x3, waiting for transfers between devices, shards(): column_values = lax.all_gather(direction, 'row', axis=1, tiled=True)  63.8 us
    dot_general x24, matrix products, work(): lax.dot_general(take_segment(column_values, column_block), block_matrix,...  58.1 us
    dot_general x24, matrix products, work(): jnp.dot(take_segment(row_values, row_block), block_matrix, precision=lax....  47.4 us
    unnamed x2, blocking collectives  41.8 us
    reduce_scatter x3, waiting for transfers between devices, shards(): lax.psum_scatter(row_image, 'col', scatter_dimension=1, tiled=True)  39.6 us
  transfers between devices with their start and end apart: 10, of which 7 were waited for; matrix products, arithmetic and copies ran while one was open for 10% of the time, Pallas kernels for 0%

commit v1 on v0

--- a/solution.py
+++ b/solution.py
@@ -112,7 +112,8 @@
     direction = innovations
     norm_now = squares(residual)
     for repeat in range(ITERS):
-        column_values = lax.all_gather(direction, "row", axis=1, tiled=True)
+        blocks = lax.all_gather(direction, "row", axis=0, tiled=False)
+        column_values = jnp.concatenate(blocks, axis=1)
         row_values = lax.all_gather(direction, "col", axis=1, tiled=True)
 
         def sweep(number, carry):

time: 873 us -> 874 us (level)
  no operation moved by 1% of the time
where the time goes in v1:
time: 874 us; the launch traced here: 870 us
  blocking collectives  305 us (35%)
  waiting for transfers between devices  285 us (33%)
  matrix products  128 us (15%)
  local copies, waits for them, and re-layouts  54.6 us (6%)
  other arithmetic  42.4 us (5%)
  loops' own time  39.5 us (5%)
  between operations  15.7 us (2%)
    reduce_scatter x3, waiting for transfers between devices, shards(): lax.psum_scatter(column_image, 'row', scatter_dimension=1, tiled=True)  179 us
    psum x3, blocking collectives, squares(): return lax.psum(jnp.sum(residual * residual, axis=1), ('row', 'col'))  118 us
    psum x2, blocking collectives, shards(): lax.psum(jnp.sum(direction * image, axis=1), ('row', 'col'))  79.7 us
    all_gather x3, waiting for transfers between devices, shards(): blocks = lax.all_gather(direction, 'row', axis=0, tiled=False)  63.9 us
    dot_general x24, matrix products, work(): lax.dot_general(take_segment(column_values, column_block), block_matrix,...  56.2 us
    dot_general x24, matrix products, work(): jnp.dot(take_segment(row_values, row_block), block_matrix, precision=lax....  47.4 us
    unnamed x2, blocking collectives  41.8 us
    reduce_scatter x3, waiting for transfers between devices, shards(): lax.psum_scatter(row_image, 'col', scatter_dimension=1, tiled=True)  39.7 us
  transfers between devices with their start and end apart: 10, of which 7 were waited for; matrix products, arithmetic and copies ran while one was open for 10% of the time, Pallas kernels for 0%

profile of v1, /device:TPU:0, one launch (start us, length us, event | category | flops | bytes accessed | tf_op | source)
XLA Modules:
  0.0 870.1 jit_solution(1445822795249530354)
XLA Ops:
  9.4 28.0 %all-gather.4 = f32[8,1,512]{2,1,0:T(1,128)S(1)} all-gather(f32[1,1,512]{2,1,0:T(1,128)S(1)} %bitcast.106), channel_id=1, replica_groups=mesh['row'=8,'col'=4] {'row'}, dimensions={0}, use_global_device_ids=true | all-gather | bytes 18432 | tf_op jit(solution)/shard_map/all_gather | solution.py:55
  37.4 5.2 all-gather.3
  42.6 7.5 all_gather.41
  50.0 7.5 all_gather.45
  58.2 95.6 %while.62 = (s32[]{:T(128)}, f32[2048]{0:T(1024)S(1)}, f32[4096]{0:T(1024)S(1)}, f32[8,512,512]{2,1,0:T(8,128)}, s32[8,3]{0,1:T(4,128)S(1)}, /*index=5*/f32[2048...) while((s32[]{:T(128)}, f32[2048]{0:T(1024)S(1)}, ...), condition=%wide.region_7.8_spmd, body=%wide.region_2.7_spmd.sunk | while | flops 204606480 | bytes 3716449 | solution.py:99
  61.6 2.6 multiply_add_fusion.6
  65.8 3.0 fusion.62
  73.5 2.6 multiply_add_fusion.6
  77.7 3.1 fusion.62
  85.6 2.6 multiply_add_fusion.6
  89.7 3.0 fusion.62
  97.5 2.6 multiply_add_fusion.6
  101.7 3.0 fusion.62
  109.4 2.6 multiply_add_fusion.6
  113.6 3.0 fusion.62
  121.4 2.6 multiply_add_fusion.6
  125.5 3.0 fusion.62
  133.3 2.6 multiply_add_fusion.6
  137.5 3.0 fusion.62
  145.3 2.6 multiply_add_fusion.6
  149.5 3.0 fusion.62
  155.4 49.2 %while.63 = (s32[]{:T(128)}, f32[64,2048]{1,0:T(8,128)S(1)}, f32[64,4096]{1,0:T(8,128)S(1)}, s32[8,3]{0,1:T(4,128)S(1)}, f32[64,4096]{1,0:T(8,128)S(1)}, /*index...) while((s32[]{:T(128)}, f32[64,2048]{1,0:T(8,128)S(1)}, ...), condition=%wide.region_11.12_spmd, body=%wide.region_10.11_spmd.sunk | while | flops 402718720 | bytes 2884853 | solution.py:150
  159.2 2.3 fusion.67
  171.5 2.3 fusion.67
  183.8 2.3 fusion.67
  196.1 2.3 fusion.67
  208.5 35.6 %all-reduce.1 = f32[4096]{0:T(1024)S(1)} all-reduce(f32[4096]{0:T(1024)S(1)} %get-tuple-element.564), channel_id=6, replica_groups=mesh['row'=8,'col'=4] {'row'}, use_global_device_ids=true, to_apply=%region_9.10.clone | all-reduce | flops 4096 | bytes 32768
  244.1 6.1 all-reduce
  250.4 43.9 %reduce-scatter.9.cloned.1.call-done = f32[64,512]{1,0:T(8,128)} async-done(((f32[64,4096]{1,0:T(8,128)}), f32[64,512]{1,0:T(8,128)}) %reduce-scatter.9.cloned.1.call-update) | async-done | bytes 131088 | tf_op jit(solution)/shard_map/reduce_scatter | solution.py:154
  295.4 39.8 %all-reduce.2 = (f32[64]{0:T(128)S(1)}, f32[64]{0:T(128)S(1)}) all-reduce(f32[64]{0:T(128)S(1)} %get-tuple-element.575, f32[64]{0:T(128)S(1)} %get-tuple-element.574), channel_id=1, replica_groups=mesh['row'=8,'col'=4] {'row','col'}, use_global_device_ids=true, to_apply=%region_1.2 | all-reduce | flops 128 | bytes 1024 | tf_op jit(solution)/shard_map/psum | solution.py:44
  336.4 39.3 %psum.44 = f32[64]{0:T(128)S(1)} all-reduce(f32[64]{0:T(128)S(1)} %get-tuple-element.646), channel_id=1, replica_groups=mesh['row'=8,'col'=4] {'row','col'}, use_global_device_ids=true, to_apply=%region_17.18 | all-reduce | flops 64 | bytes 512 | tf_op jit(solution)/shard_map/psum | solution.py:44
  376.5 8.2 all_gather.48
  384.7 32.0 %all-gather.14.cloned.1.call-done = f32[512,512]{1,0:T(8,128)} async-done(((f32[64,512]{1,0:T(8,128)}), f32[512,512]{1,0:T(8,128)}) %all-gather.14.cloned.1.call-update) | async-done | bytes 1048592 | tf_op jit(solution)/shard_map/all_gather | solution.py:115
  418.1 49.1 %while.64 = (s32[]{:T(128)}, f32[64,2048]{1,0:T(8,128)S(1)}, f32[64,4096]{1,0:T(8,128)S(1)}, s32[8,3]{0,1:T(4,128)S(1)}, f32[64,4096]{1,0:T(8,128)S(1)}, /*index...) while((s32[]{:T(128)}, f32[64,2048]{1,0:T(8,128)S(1)}, ...), condition=%wide.region_19.20_spmd, body=%wide.region_18.19_spmd.sunk | while | flops 402718720 | bytes 2884853 | solution.py:150
  464.9 2.3 fusion.73
  468.9 19.7 %reduce-scatter.11.cloned.1.call-done = f32[64,512]{1,0:T(8,128)} async-done(((f32[64,2048]{1,0:T(8,128)}), f32[64,512]{1,0:T(8,128)}) %reduce-scatter.11.cloned.1.call-update) | async-done | bytes 131088 | tf_op jit(solution)/shard_map/reduce_scatter | solution.py:153
  488.6 68.0 %reduce-scatter.13.cloned.1.call-done = f32[64,512]{1,0:T(8,128)} async-done(((f32[64,4096]{1,0:T(8,128)}), f32[64,512]{1,0:T(8,128)}) %reduce-scatter.13.cloned.1.call-update) | async-done | bytes 131088 | tf_op jit(solution)/shard_map/reduce_scatter | solution.py:154
  557.7 39.9 %psum.45 = f32[64]{0:T(128)S(1)} all-reduce(f32[64]{0:T(128)S(1)} %multiply_reduce_fusion.4), channel_id=1, replica_groups=mesh['row'=8,'col'=4] {'row','col'}, use_global_device_ids=true, to_apply=%region_23.24 | all-reduce | flops 64 | bytes 512 | tf_op jit(solution)/shard_map/psum | solution.py:156
  599.4 39.2 %psum.46 = f32[64]{0:T(128)S(1)} all-reduce(f32[64]{0:T(128)S(1)} %get-tuple-element.644), channel_id=1, replica_groups=mesh['row'=8,'col'=4] {'row','col'}, use_global_device_ids=true, to_apply=%region_25.26 | all-reduce | flops 64 | bytes 512 | tf_op jit(solution)/shard_map/psum | solution.py:44
  640.2 8.3 all_gather.51
  648.5 31.8 %all-gather.16.cloned.1.call-done = f32[512,512]{1,0:T(8,128)} async-done(((f32[64,512]{1,0:T(8,128)}), f32[512,512]{1,0:T(8,128)}) %all-gather.16.cloned.1.call-update) | async-done | bytes 1048592 | tf_op jit(solution)/shard_map/all_gather | solution.py:115
  681.8 49.1 %while.65 = (s32[]{:T(128)}, f32[64,2048]{1,0:T(8,128)S(1)}, f32[64,4096]{1,0:T(8,128)S(1)}, s32[8,3]{0,1:T(4,128)S(1)}, f32[64,4096]{1,0:T(8,128)S(1)}, /*index...) while((s32[]{:T(128)}, f32[64,2048]{1,0:T(8,128)S(1)}, ...), condition=%wide.region_27.28_spmd, body=%wide.region_26.27_spmd.sunk | while | flops 402718720 | bytes 2884853 | solution.py:150
  691.8 2.3 fusion.79
  704.0 2.3 fusion.79
  728.6 2.3 fusion.79
  732.4 19.9 %reduce-scatter.15.cloned.1.call-done = f32[64,512]{1,0:T(8,128)} async-done(((f32[64,2048]{1,0:T(8,128)}), f32[64,512]{1,0:T(8,128)}) %reduce-scatter.15.cloned.1.call-update) | async-done | bytes 131088 | tf_op jit(solution)/shard_map/reduce_scatter | solution.py:153
  752.3 67.4 %reduce-scatter.17.cloned.1.call-done = f32[64,512]{1,0:T(8,128)} async-done(((f32[64,4096]{1,0:T(8,128)}), f32[64,512]{1,0:T(8,128)}) %reduce-scatter.17.cloned.1.call-update) | async-done | bytes 131088 | tf_op jit(solution)/shard_map/reduce_scatter | solution.py:154
  820.9 39.9 %psum.47 = f32[64]{0:T(128)S(1)} all-reduce(f32[64]{0:T(128)S(1)} %multiply_reduce_fusion.2), channel_id=1, replica_groups=mesh['row'=8,'col'=4] {'row','col'}, use_global_device_ids=true, to_apply=%region_31.32 | all-reduce | flops 64 | bytes 512 | tf_op jit(solution)/shard_map/psum | solution.py:156
  (204 shorter events, 163.8 us)
Async XLA Ops:
  7.2 51.0 %all-gather.10.cloned.1.call-start = ((), (), s32[]{:S(2)}) async-start(), calls=%async_computation.6 | async-start | bytes 1179648 | tf_op jit(solution)/shard_map/all_gather | solution.py:54
  7.9 146.0 %all-gather.12.cloned.1.call-start = ((), (), s32[]{:S(2)}) async-start(), calls=%async_computation.13 | async-start | bytes 1179648 | tf_op jit(solution)/shard_map/all_gather | solution.py:115
  8.6 241.7 %reduce-scatter.7.cloned.1.call-start = ((), (), s32[]{:S(2)}) async-start(), calls=%async_computation.7 | async-start | bytes 655360 | tf_op jit(solution)/shard_map/reduce_scatter | solution.py:153
  155.3 50.8 %copy-start.12 = (u32[32]{0:T(128)S(1)}, u32[32]{0:T(128)}, u32[]{:S(2)}) copy-start(u32[32]{0:T(128)} %constant.217) | copy-start | bytes 388
  155.3 51.3 %copy-start.11 = (u32[32]{0:T(128)S(1)}, u32[32]{0:T(128)}, u32[]{:S(2)}) copy-start(u32[32]{0:T(128)} %constant.221) | copy-start | bytes 388
  155.3 95.0 %copy-start.10 = (f32[512]{0:T(512)S(1)}, f32[512]{0:T(512)}, u32[]{:S(2)}) copy-start(f32[512]{0:T(512)} %param.17) | copy-start | bytes 6148
  155.3 139.0 %copy-start.7 = (f32[64,512]{1,0:T(8,128)S(1)}, f32[64,512]{1,0:T(8,128)}, u32[]{:S(2)}) copy-start(f32[64,512]{1,0:T(8,128)} %param.14) | copy-start | bytes 393220
  204.6 0.8 copy-start.5
  204.6 1.2 copy-start.1
  205.4 88.9 %reduce-scatter.9.cloned.1.call-start = ((), (), s32[]{:S(2)}) async-start(), calls=%async_computation.8 | async-start | bytes 1179648 | tf_op jit(solution)/shard_map/reduce_scatter | solution.py:154
  206.0 210.7 %all-gather.14.cloned.1.call-start = ((), (), s32[]{:S(2)}) async-start(), calls=%async_computation.14 | async-start | bytes 1179648 | tf_op jit(solution)/shard_map/all_gather | solution.py:115
  375.7 42.3 %copy-start.13 = (f32[64]{0:T(128)}, f32[64]{0:T(128)S(1)}, u32[]{:S(2)}) copy-start(f32[64]{0:T(128)S(1)} %psum.44) | copy-start | bytes 772
  376.5 112.1 %reduce-scatter.11.cloned.1.call-start = ((), (), s32[]{:S(2)}) async-start(), calls=%async_computation.9 | async-start | bytes 655360 | tf_op jit(solution)/shard_map/reduce_scatter | solution.py:153
  418.1 138.5 %copy-start.3 = (f32[64,512]{1,0:T(8,128)S(1)}, f32[64,512]{1,0:T(8,128)}, u32[]{:S(2)}) copy-start(f32[64,512]{1,0:T(8,128)} %multiply_add_fusion.4) | copy-start | bytes 393220
  467.3 0.8 copy-start.6
  467.3 1.2 copy-start.2
  468.1 88.5 %reduce-scatter.13.cloned.1.call-start = ((), (), s32[]{:S(2)}) async-start(), calls=%async_computation.10 | async-start | bytes 1179648 | tf_op jit(solution)/shard_map/reduce_scatter | solution.py:154
  468.8 211.5 %all-gather.16.cloned.1.call-start = ((), (), s32[]{:S(2)}) async-start(), calls=%async_computation.15 | async-start | bytes 1179648 | tf_op jit(solution)/shard_map/all_gather | solution.py:115
  599.4 82.3 %copy-start.9 = (f32[64,512]{1,0:T(8,128)}, f32[64,512]{1,0:T(8,128)S(1)}, u32[]{:S(2)}) copy-start(f32[64,512]{1,0:T(8,128)S(1)} %get-tuple-element.645) | copy-start | bytes 393220
  638.7 43.0 %copy-start.14 = (f32[64]{0:T(128)}, f32[64]{0:T(128)S(1)}, u32[]{:S(2)}) copy-start(f32[64]{0:T(128)S(1)} %psum.46) | copy-start | bytes 772
  640.1 112.2 %reduce-scatter.15.cloned.1.call-start = ((), (), s32[]{:S(2)}) async-start(), calls=%async_computation.11 | async-start | bytes 655360 | tf_op jit(solution)/shard_map/reduce_scatter | solution.py:153
  681.8 138.0 %copy-start.8 = (f32[64,512]{1,0:T(8,128)S(1)}, f32[64,512]{1,0:T(8,128)}, u32[]{:S(2)}) copy-start(f32[64,512]{1,0:T(8,128)} %multiply_add_fusion.3) | copy-start | bytes 393220
  731.0 0.8 copy-start.4
  731.0 1.2 copy-start
  731.8 88.0 %reduce-scatter.17.cloned.1.call-start = ((), (), s32[]{:S(2)}) async-start(), calls=%async_computation.12 | async-start | bytes 1179648 | tf_op jit(solution)/shard_map/reduce_scatter | solution.py:154
Sparse Core Ops, SparseCore 0:
  10.2 42.9 all-gather.9
  55.3 39.1 all-gather.11
  205.5 20.9 reduce-scatter.6
  229.8 64.4 reduce-scatter.8
  376.6 40.0 all-gather.13
  468.2 20.3 reduce-scatter.10
  492.0 64.5 reduce-scatter.12
  640.2 40.0 all-gather.15
  731.9 20.3 reduce-scatter.14
  755.6 64.1 reduce-scatter.16
